TPU v7x, 32 devices: a whole 2x2x4 slice. The times are simulated.
32 devices in a mesh: row: 8 (over z, y), col: 4 (over x, core).
Axes of the slice: x: 2, y: 2, z: 4, core: 2. Of those that a mesh axis runs over, the one named last changes fastest.
Arguments:
- activations: bfloat16 [512, 28672], P('col', 'row'), may hold values from -36 to 36
- output_gradient: bfloat16 [512, 8192], P('row', 'col'), may hold values from -6 to 6
- frozen_weight: bfloat16 [28672, 8192], P('row', 'col'), may hold values from -0.0390625 to 0.0390625
- sparsity_mask_pattern: int32 [7168, 8192], P('row', 'col'), may hold values from 0 to 5
- adapter_left_factor: bfloat16 [28672, 16], P('row'), may hold values from -0.19921875 to 0.19921875
- adapter_right_factor: bfloat16 [16, 8192], P(None, 'col'), may hold values from -0.359375 to 0.359375
Outputs:
- input_grad: bfloat16 [512, 28672], P('col', 'row')
- left_grad: float32 [28672, 16], P('row')
- right_grad: float32 [16, 8192], P(None, 'col')
Inputs may be any that keep to these rules, and one draw needn't show every extreme that they name: `sparsity_mask_pattern`: a pattern number of the 2:4 mask.
All inputs are finite; a program needn't handle non-finite values.
Results may differ from a plain program's by a relative error of at most 0.005.
Values may be sent and summed in bfloat16 or wider, within the bound.
No kernel may reach another device: no remote copies, remote signals or barrier semaphores. Data moves between devices by JAX's collectives and lax.ppermute only.
A program may use at most 192 MiB of HBM per device.

v0:
```python
import jax
import jax.numpy as jnp
from jax import lax
from jax.sharding import PartitionSpec as P

PAIRS = ((0, 1), (0, 2), (0, 3), (1, 2), (1, 3), (2, 3))
ADAPTER_SCALE = 2.0


def expand_mask(code):
    groups = []
    for column in range(4):
        kept = jnp.zeros(code.shape, jnp.float32)
        for pattern in range(6):
            if column in PAIRS[pattern]:
                kept = kept + (code == pattern).astype(jnp.float32)
        groups.append(kept)
    stacked = jnp.stack(groups, axis=1)
    return stacked.reshape(code.shape[0] * 4, code.shape[1])


def input_sums_of(grad_rows, merged):
    return lax.psum_scatter(
        lax.dot_general(
            grad_rows, merged, (((1,), (1,)), ((), ())), preferred_element_type=jnp.float32
        ),
        "col",
        scatter_dimension=0,
        tiled=True,
    )


def weight_grad_of(activations, grad_rows):
    return lax.dot_general(
        lax.all_gather(activations, "col", axis=0, tiled=True),
        grad_rows,
        (((0,), (0,)), ((), ())),
        preferred_element_type=jnp.float32,
    )


def per_device(
    activations,
    output_gradient,
    frozen_weight,
    sparsity_mask_pattern,
    adapter_left_factor,
    adapter_right_factor,
):
    masked = expand_mask(sparsity_mask_pattern)
    low_rank_update = jnp.dot(
        adapter_left_factor, adapter_right_factor, preferred_element_type=jnp.float32
    )
    merged = (
        masked * (frozen_weight.astype(jnp.float32) + ADAPTER_SCALE * low_rank_update)
    ).astype(jnp.bfloat16)
    grad_rows = lax.all_gather(output_gradient, "row", axis=0, tiled=True)
    all_tokens = grad_rows.shape[0]
    first_grad = weight_grad_of(activations, grad_rows)
    weight_grad, later_grads = lax.optimization_barrier((first_grad, grad_rows))
    input_grad = input_sums_of(later_grads, merged).astype(jnp.bfloat16)
    pruned_gradient = (masked * weight_grad / all_tokens).astype(jnp.bfloat16)
    left_partial = ADAPTER_SCALE * lax.dot_general(
        pruned_gradient,
        adapter_right_factor,
        (((1,), (1,)), ((), ())),
        preferred_element_type=jnp.float32,
    )
    right_partial = ADAPTER_SCALE * lax.dot_general(
        adapter_left_factor,
        pruned_gradient,
        (((0,), (0,)), ((), ())),
        preferred_element_type=jnp.float32,
    )
    right_grad = lax.psum(right_partial, "row")
    left_grad = lax.psum(left_partial, "col")
    return (input_grad, left_grad, right_grad)


def solution(mesh):
    in_specs = (
        P("col", "row"),
        P("row", "col"),
        P("row", "col"),
        P("row", "col"),
        P("row", None),
        P(None, "col"),
    )
    out_specs = (P("col", "row"), P("row", None), P(None, "col"))
    return jax.shard_map(
        per_device, mesh=mesh, in_specs=in_specs, out_specs=out_specs, check_vma=False
    )
```

profile of v0, /device:TPU:0, one launch (start us, length us, event | category | flops | bytes accessed | tf_op | source)
XLA Modules:
  0.0 334.8 jit_solution(17214782488458227821)
XLA Ops:
  7.2 0.7 all-gather.5.cloned.1.call-update
  7.9 0.0 all-gather.3.cloned.1.call-start
  8.0 0.7 all-gather.3.cloned.1.call-update
  8.7 0.0 reduce-scatter.2.cloned.1.call-start
  8.7 7.8 %fusion = (f32[896,1,2048]{2,0,1:T(8,128)S(1)}, pred[896,2048]{1,0:T(8,128)(4,1)S(1)}, pred[896,2048]{1,0:T(8,128)(4,1)S(1)}, pred[896,2048]{1,0:T(8,128)(4,1)}) fusion(s32[896,2048]{1,0:T(8,128)} %param.9), kind=kLoop, calls=%fused_computation.11 | loop fusion | flops 14680064 | bytes 20185088 | tf_op jit(solution)/shard_map/stack | solution.py:18
  16.6 6.5 %fusion.1 = (f32[896,1,2048]{2,0,1:T(8,128)S(1)}, pred[896,2048]{1,0:T(8,128)(4,1)S(1)}, pred[896,2048]{1,0:T(8,128)(4,1)}) fusion(pred[896,2048]{1,0:T(8,128)(4,1)S(1)} %get-tuple-element.8, s32[896,2048]{1,0:T(8,128)} %param.9), kind=kLoop, calls=%fused_computation.12 | loop fusion | flops 12845056 | bytes 20185088 | tf_op jit(solution)/shard_map/stack | solution.py:18
  23.1 3.6 %fusion.2 = (f32[896,1,2048]{2,0,1:T(8,128)S(1)}, pred[896,2048]{1,0:T(8,128)(4,1)}) fusion(pred[896,2048]{1,0:T(8,128)(4,1)S(1)} %get-tuple-element.12, pred[896,2048]{1,0:T(8,128)(4,1)S(1)} %get-tuple-element.9, s32[896,2048]{1,0:T(8,128)S(1)} %bitcast.20), kind=kLoop, calls=%fused_computation.13 | loop fusion | flops 11010048 | bytes 20185088 | tf_op jit(solution)/shard_map/stack | solution.py:18
  26.7 5.1 %fusion.3 = f32[896,1,2048]{2,0,1:T(8,128)S(1)} fusion(pred[896,2048]{1,0:T(8,128)(4,1)} %get-tuple-element.15, pred[896,2048]{1,0:T(8,128)(4,1)} %get-tuple-element.13, pred[896,2048]{1,0:T(8,128)(4,1)} %get-tuple-element.10), kind=kLoop, calls=%fused_computation.14 | loop fusion | flops 9175040 | bytes 12845056 | tf_op jit(solution)/shard_map/stack | solution.py:18
  31.8 10.3 %pad_maximum_fusion = f32[896,4,2048]{2,0,1:T(8,128)} fusion(f32[896,1,2048]{2,0,1:T(8,128)S(1)} %fusion.3, f32[896,1,2048]{2,0,1:T(8,128)S(1)} %get-tuple-element.14, f32[896,1,2048]{2,0,1:T(8,128)S(1)} %get-tuple-element.11, f32[896,1,2048]{2,0,1:T(8,128)S(1)} %get-tuple-element.7), kind=kLoop, calls=%fused_computation | loop fusion | flops 22020096 | bytes 58720256 | tf_op jit(solution)/shard_map/stack | solution.py:18
  42.1 33.6 %copy.9 = f32[896,4,2048]{2,1,0:T(4,128)} copy(f32[896,4,2048]{2,0,1:T(8,128)} %pad_maximum_fusion) | data formatting | bytes 58720256 | tf_op jit(solution)/shard_map/stack | solution.py:18
  75.7 33.5 %reshape.9 = f32[3584,2048]{1,0:T(8,128)} reshape(f32[896,4,2048]{2,1,0:T(4,128)} %copy.9) | data formatting | bytes 58720256 | tf_op jit(solution)/shard_map/reshape | solution.py:19
  109.2 16.2 %fusion.7 = f32[3584,2048]{1,0:T(8,128)} fusion(bf16[512,3584]{1,0:T(8,128)(2,1)} %all-gather.3.cloned.1.call-done, bf16[512,2048]{1,0:T(8,128)(2,1)} %all-gather.5.cloned.1.call-done), kind=kOutput, calls=%fused_computation.26 | convolution fusion | flops 7516192768 | bytes 35127296 | tf_op jit(solution)/shard_map/dot_general | solution.py:34
  125.4 21.5 %fusion.4 = f32[512,3584]{1,0:T(8,128)} fusion(bf16[512,2048]{1,0:T(8,128)(2,1)S(1)} %copy-done.2, f32[3584,2048]{1,0:T(8,128)} %reshape.9, bf16[3584,2048]{1,0:T(8,128)(2,1)} %param.8, bf16[3584,16]{0,1:T(8,128)(2,1)S(1)} %copy-done, bf16[16,2048]{1,0:T(8,128)(2,1)S(1)} %copy-done.1), kind=kOutput, calls=%fused_computation.22 | convolution fusion | flops 7787773952 | bytes 53657600 | tf_op jit(solution)/shard_map/dot_general | solution.py:24
  147.0 0.0 all-reduce.3.cloned.1.call-start
  147.0 26.9 %multiply_convert_fusion = bf16[3584,2048]{1,0:T(8,128)(2,1)} fusion(f32[3584,2048]{1,0:T(8,128)} %reshape.9, f32[3584,2048]{1,0:T(8,128)} %fusion.7), kind=kLoop, calls=%fused_computation.1 | loop fusion | flops 22020096 | bytes 73400320 | tf_op jit(solution)/shard_map/convert_element_type | solution.py:62
  173.9 9.9 %convolution_multiply_fusion = f32[3584,16]{0,1:T(8,128)} fusion(bf16[3584,2048]{1,0:T(8,128)(2,1)} %multiply_convert_fusion, bf16[16,2048]{1,0:T(8,128)(2,1)S(1)} %copy-done.1), kind=kOutput, calls=%fused_computation.15 | convolution fusion | flops 234938368 | bytes 14974976 | tf_op jit(solution)/shard_map/dot_general | solution.py:63
  183.8 0.0 all-reduce.5.cloned.1.call-start
  183.9 8.0 %fusion.5 = f32[16,2048]{1,0:T(8,128)} fusion(bf16[3584,16]{0,1:T(8,128)(2,1)S(1)} %copy-done, bf16[3584,2048]{1,0:T(8,128)(2,1)} %multiply_convert_fusion), kind=kOutput, calls=%fused_computation.24 | convolution fusion | flops 234913792 | bytes 14925824 | tf_op jit(solution)/shard_map/dot_general | solution.py:69
  191.9 24.0 %reduce-scatter.2.cloned.1.call-done = f32[128,3584]{1,0:T(8,128)} async-done(((f32[512,3584]{1,0:T(8,128)}), f32[128,3584]{1,0:T(8,128)}) %reduce-scatter.2.cloned.1.call-update) | async-done | bytes 1835024 | tf_op jit(solution)/shard_map/reduce_scatter | solution.py:23
  215.9 2.5 convert_element_type.44
  218.4 32.5 %all-reduce.3.cloned.1.call-done = f32[3584,16]{0,1:T(8,128)} async-done(((f32[3584,16]{0,1:T(8,128)}), f32[3584,16]{0,1:T(8,128)}) %all-reduce.3.cloned.1.call-update) | async-done | bytes 229392 | tf_op jit(solution)/shard_map/psum | solution.py:76
  250.9 74.2 %all-reduce.5.cloned.1.call-done = f32[16,2048]{1,0:T(8,128)} async-done(((f32[16,2048]{1,0:T(8,128)}), f32[16,2048]{1,0:T(8,128)}) %all-reduce.5.cloned.1.call-update) | async-done | bytes 131088 | tf_op jit(solution)/shard_map/psum | solution.py:75
  325.0 1.6 copy.12
  326.7 1.6 copy.13
  (17 shorter events, 0.1 us)
Async XLA Ops:
  7.2 118.2 %copy-start = (bf16[3584,16]{0,1:T(8,128)(2,1)S(1)}, bf16[3584,16]{0,1:T(8,128)(2,1)}, u32[]{:S(2)}) copy-start(bf16[3584,16]{0,1:T(8,128)(2,1)} %param.10) | copy-start | bytes 344068
  7.2 102.0 %all-gather.5.cloned.1.call-start = ((), (), s32[]{:S(2)}) async-start(), calls=%async_computation.2 | async-start | bytes 2359296 | tf_op jit(solution)/shard_map/all_gather | solution.py:57
  7.9 101.3 %all-gather.3.cloned.1.call-start = ((), (), s32[]{:S(2)}) async-start(), calls=%async_computation.1 | async-start | bytes 4587520 | tf_op jit(solution)/shard_map/all_gather | solution.py:35
  8.7 207.2 %reduce-scatter.2.cloned.1.call-start = ((), (), s32[]{:S(2)}) async-start(), calls=%async_computation.3 | async-start | bytes 9175040 | tf_op jit(solution)/shard_map/reduce_scatter | solution.py:23
  8.7 14.4 %slice-start = ((s8[7340032]{0:T(1024)(128)(4,1)}), s8[4194304]{0:T(1024)(128)(4,1)S(1)}, s32[]{:S(2)}) async-start(s8[7340032]{0:T(1024)(128)(4,1)} %bitcast.19), calls=%async_computation.6 | async-start | bytes 8388608
  16.5 6.5 %slice-start.1 = ((s8[7340032]{0:T(1024)(128)(4,1)}), s8[3145728]{0:T(1024)(128)(4,1)S(1)}, s32[]{:S(2)}) async-start(s8[7340032]{0:T(1024)(128)(4,1)} %bitcast.19), calls=%async_computation.7 | async-start | bytes 6291456
  109.2 16.2 %copy-start.1 = (bf16[16,2048]{1,0:T(8,128)(2,1)S(1)}, bf16[16,2048]{1,0:T(8,128)(2,1)}, u32[]{:S(2)}) copy-start(bf16[16,2048]{1,0:T(8,128)(2,1)} %param.11) | copy-start | bytes 196612
  109.2 16.2 %copy-start.2 = (bf16[512,2048]{1,0:T(8,128)(2,1)S(1)}, bf16[512,2048]{1,0:T(8,128)(2,1)}, u32[]{:S(2)}) copy-start(bf16[512,2048]{1,0:T(8,128)(2,1)} %all-gather.5.cloned.1.call-done) | copy-start | bytes 6291460
  147.0 103.9 %all-reduce.3.cloned.1.call-start = ((), (), s32[]{:S(2)}) async-start(), calls=%async_computation.4 | async-start | bytes 458752 | tf_op jit(solution)/shard_map/psum | solution.py:76
  183.8 141.2 %all-reduce.5.cloned.1.call-start = ((), (), s32[]{:S(2)}) async-start(), calls=%async_computation.5 | async-start | bytes 262144 | tf_op jit(solution)/shard_map/psum | solution.py:75
Sparse Core Ops, SparseCore 0:
  10.1 51.8 all-gather.4
  63.5 29.9 all-gather.2
  147.1 68.7 reduce-scatter.1
  218.6 32.1 all-reduce.2
  254.6 70.3 all-reduce.4
where the time goes:
time: 336 us; the launch traced here: 335 us
  waiting for transfers between devices  132 us (39%)
  local copies, waits for them, and re-layouts  70.4 us (21%)
  other arithmetic  62.8 us (19%)
  matrix products  55.6 us (17%)
  between operations  13.8 us (4%)
    psum x1, waiting for transfers between devices, per_device(): right_grad = lax.psum(right_partial, 'row')  74.2 us
    another operation x1, local copies, waits for them, and re-layouts, expand_mask(): stacked = jnp.stack(groups, axis=1)  33.6 us
    reshape x1, local copies, waits for them, and re-layouts, expand_mask(): return stacked.reshape(code.shape[0] * 4, code.shape[1])  33.5 us
    another operation x5, other arithmetic, expand_mask(): stacked = jnp.stack(groups, axis=1)  33.3 us
    psum x1, waiting for transfers between devices, per_device(): left_grad = lax.psum(left_partial, 'col')  32.5 us
    convert_element_type x1, other arithmetic, per_device(): pruned_gradient = (masked * weight_grad / all_tokens).astype(jnp.bfloat16)  26.9 us
    reduce_scatter x1, waiting for transfers between devices, input_sums_of(): lax.psum_scatter(lax.dot_general(grad_rows, merged, (((1,), (1,)), ((), (...  24 us
    dot_general x1, matrix products, input_sums_of(): lax.dot_general(grad_rows, merged, (((1,), (1,)), ((), ())), preferred_el...  21.5 us
  transfers between devices with their start and end apart: 5, of which 3 were waited for; matrix products, arithmetic and copies ran while one was open for 44% of the time, Pallas kernels for 0%

commit v1 on v0

--- a/solution.py
+++ b/solution.py
@@ -73,7 +73,11 @@
         preferred_element_type=jnp.float32,
     )
     right_grad = lax.psum(right_partial, "row")
-    left_grad = lax.psum(left_partial, "col")
+    left_grad = left_partial
+    for hop in (1, 2):
+        left_grad = left_grad + lax.ppermute(
+            left_grad, "col", [(dev, dev ^ hop) for dev in range(4)]
+        )
     return (input_grad, left_grad, right_grad)
 
 

time: 336 us -> 304 us (0.905)
  waiting for transfers between devices: 132 us -> 103 us
  matrix products: 55.6 us -> 49.6 us
  starting transfers between devices: 0.2 us -> 4.14 us
    psum x1 -> x0, waiting for transfers between devices: 32.5 us -> none  [per_device(): left_grad = lax.psum(left_partial, 'col')]
    ppermute x0 -> x2, waiting for transfers between devices: none -> 9.65 us  [per_device(): lax.ppermute(left_grad, 'col', [(dev, dev ^ hop) for dev in range(4)])]
    dot_general x1, matrix products: 8 us -> 2.66 us  [per_device(): lax.dot_general(adapter_left_factor, pruned_gradient, (((0,), (0,)), ((),...]
    ppermute x0 -> x2, starting transfers between devices: none -> 3.98 us  [per_device(): lax.ppermute(left_grad, 'col', [(dev, dev ^ hop) for dev in range(4)])]
    reduce_scatter x1, waiting for transfers between devices: 24 us -> 20.1 us  [input_sums_of(): lax.psum_scatter(lax.dot_general(grad_rows, merged, (((1,), (1,)), ((), (...]
  transfers between devices with their start and end apart: 5 -> 6, of which waited for: 3 -> 4; matrix products, arithmetic and copies ran while one was open for 44% -> 47% of each run, Pallas kernels for 0% -> 0%
where the time goes in v1:
time: 304 us; the launch traced here: 303 us
  waiting for transfers between devices  103 us (34%)
  local copies, waits for them, and re-layouts  68.7 us (23%)
  other arithmetic  63.9 us (21%)
  matrix products  49.6 us (16%)
  between operations  13.8 us (5%)
  starting transfers between devices  4.14 us (1%)
    psum x1, waiting for transfers between devices, per_device(): right_grad = lax.psum(right_partial, 'row')  71.7 us
    another operation x1, local copies, waits for them, and re-layouts, expand_mask(): stacked = jnp.stack(groups, axis=1)  33.6 us
    reshape x1, local copies, waits for them, and re-layouts, expand_mask(): return stacked.reshape(code.shape[0] * 4, code.shape[1])  33.5 us
    another operation x5, other arithmetic, expand_mask(): stacked = jnp.stack(groups, axis=1)  33.3 us
    convert_element_type x1, other arithmetic, per_device(): pruned_gradient = (masked * weight_grad / all_tokens).astype(jnp.bfloat16)  27.3 us
    dot_general x1, matrix products, input_sums_of(): lax.dot_general(grad_rows, merged, (((1,), (1,)), ((), ())), preferred_el...  21.5 us
    reduce_scatter x1, waiting for transfers between devices, input_sums_of(): lax.psum_scatter(lax.dot_general(grad_rows, merged, (((1,), (1,)), ((), (...  20.1 us
    dot_general x1, matrix products, weight_grad_of(): lax.dot_general(lax.all_gather(activations, 'col', axis=0, tiled=True), g...  16.2 us
  transfers between devices with their start and end apart: 6, of which 4 were waited for; matrix products, arithmetic and copies ran while one was open for 47% of the time, Pallas kernels for 0%

profile of v1, /device:TPU:0, one launch (start us, length us, event | category | flops | bytes accessed | tf_op | source)
XLA Modules:
  0.0 303.1 jit_solution(3380820587304936236)
XLA Ops:
  7.2 0.7 all-gather.5.cloned.1.call-update
  8.0 0.7 all-gather.3.cloned.1.call-update
  8.7 7.8 %fusion = (f32[896,1,2048]{2,0,1:T(8,128)S(1)}, pred[896,2048]{1,0:T(8,128)(4,1)S(1)}, pred[896,2048]{1,0:T(8,128)(4,1)S(1)}, pred[896,2048]{1,0:T(8,128)(4,1)}) fusion(s32[896,2048]{1,0:T(8,128)} %param.9), kind=kLoop, calls=%fused_computation.11 | loop fusion | flops 14680064 | bytes 20185088 | tf_op jit(solution)/shard_map/stack | solution.py:18
  16.5 6.5 %fusion.1 = (f32[896,1,2048]{2,0,1:T(8,128)S(1)}, pred[896,2048]{1,0:T(8,128)(4,1)S(1)}, pred[896,2048]{1,0:T(8,128)(4,1)}) fusion(pred[896,2048]{1,0:T(8,128)(4,1)S(1)} %get-tuple-element.8, s32[896,2048]{1,0:T(8,128)} %param.9), kind=kLoop, calls=%fused_computation.12 | loop fusion | flops 12845056 | bytes 20185088 | tf_op jit(solution)/shard_map/stack | solution.py:18
  23.0 3.6 %fusion.2 = (f32[896,1,2048]{2,0,1:T(8,128)S(1)}, pred[896,2048]{1,0:T(8,128)(4,1)}) fusion(pred[896,2048]{1,0:T(8,128)(4,1)S(1)} %get-tuple-element.12, pred[896,2048]{1,0:T(8,128)(4,1)S(1)} %get-tuple-element.9, s32[896,2048]{1,0:T(8,128)S(1)} %bitcast.20), kind=kLoop, calls=%fused_computation.13 | loop fusion | flops 11010048 | bytes 20185088 | tf_op jit(solution)/shard_map/stack | solution.py:18
  26.7 5.1 %fusion.3 = f32[896,1,2048]{2,0,1:T(8,128)S(1)} fusion(pred[896,2048]{1,0:T(8,128)(4,1)} %get-tuple-element.15, pred[896,2048]{1,0:T(8,128)(4,1)} %get-tuple-element.13, pred[896,2048]{1,0:T(8,128)(4,1)} %get-tuple-element.10), kind=kLoop, calls=%fused_computation.14 | loop fusion | flops 9175040 | bytes 12845056 | tf_op jit(solution)/shard_map/stack | solution.py:18
  31.8 10.3 %pad_maximum_fusion = f32[896,4,2048]{2,0,1:T(8,128)} fusion(f32[896,1,2048]{2,0,1:T(8,128)S(1)} %fusion.3, f32[896,1,2048]{2,0,1:T(8,128)S(1)} %get-tuple-element.14, f32[896,1,2048]{2,0,1:T(8,128)S(1)} %get-tuple-element.11, f32[896,1,2048]{2,0,1:T(8,128)S(1)} %get-tuple-element.7), kind=kLoop, calls=%fused_computation | loop fusion | flops 22020096 | bytes 58720256 | tf_op jit(solution)/shard_map/stack | solution.py:18
  42.0 33.6 %copy.9 = f32[896,4,2048]{2,1,0:T(4,128)} copy(f32[896,4,2048]{2,0,1:T(8,128)} %pad_maximum_fusion) | data formatting | bytes 58720256 | tf_op jit(solution)/shard_map/stack | solution.py:18
  75.6 33.5 %reshape.9 = f32[3584,2048]{1,0:T(8,128)} reshape(f32[896,4,2048]{2,1,0:T(4,128)} %copy.9) | data formatting | bytes 58720256 | tf_op jit(solution)/shard_map/reshape | solution.py:19
  109.2 16.2 %fusion.7 = f32[3584,2048]{1,0:T(8,128)} fusion(bf16[512,3584]{1,0:T(8,128)(2,1)} %all-gather.3.cloned.1.call-done, bf16[512,2048]{1,0:T(8,128)(2,1)} %all-gather.5.cloned.1.call-done), kind=kOutput, calls=%fused_computation.26 | convolution fusion | flops 7516192768 | bytes 35127296 | tf_op jit(solution)/shard_map/dot_general | solution.py:34
  125.4 21.5 %fusion.4 = f32[512,3584]{1,0:T(8,128)} fusion(bf16[512,2048]{1,0:T(8,128)(2,1)S(1)} %copy-done.3, f32[3584,2048]{1,0:T(8,128)} %reshape.9, bf16[3584,2048]{1,0:T(8,128)(2,1)} %param.8, bf16[3584,16]{0,1:T(8,128)(2,1)S(1)} %copy-done, bf16[16,2048]{1,0:T(8,128)(2,1)S(1)} %copy-done.2), kind=kOutput, calls=%fused_computation.22 | convolution fusion | flops 7787773952 | bytes 53657600 | tf_op jit(solution)/shard_map/dot_general | solution.py:24
  147.0 0.0 all-reduce.2.cloned.1.call-start
  147.0 27.3 %multiply_convert_fusion = bf16[3584,2048]{1,0:T(8,128)(2,1)} fusion(f32[3584,2048]{1,0:T(8,128)} %reshape.9, f32[3584,2048]{1,0:T(8,128)} %fusion.7), kind=kLoop, calls=%fused_computation.1 | loop fusion | flops 22020096 | bytes 73400320 | tf_op jit(solution)/shard_map/convert_element_type | solution.py:62
  174.4 9.2 %convolution_multiply_fusion = f32[3584,16]{0,1:T(8,128)S(1)} fusion(bf16[3584,2048]{1,0:T(8,128)(2,1)} %multiply_convert_fusion, bf16[16,2048]{1,0:T(8,128)(2,1)S(1)} %copy-done.2), kind=kOutput, calls=%fused_computation.15 | convolution fusion | flops 234938368 | bytes 14974976 | tf_op jit(solution)/shard_map/dot_general | solution.py:63
  183.6 0.4 collective-permute-start
  184.0 1.1 collective-permute-done
  185.1 3.6 %collective-permute-start.1 = (f32[3584,16]{0,1:T(8,128)S(1)}, f32[3584,16]{0,1:T(8,128)S(1)}, u32[]{:S(2)}, u32[]{:S(2)}) collective-permute-start(f32[3584,16]{0,1:T(8,128)S(1)} %add.46), channel_id=1, source_target_pairs={{0,2},{1,3},{2,0},{3,1},{4,6},{5,7},{6,4},{7,5},{8,10},{9,11},{10,... | collective-permute-start | bytes 688136 | tf_op jit(solution)/shard_map/ppermute | solution.py:78
  188.7 2.7 fusion.5
  191.4 8.5 %collective-permute-done.1 = f32[3584,16]{0,1:T(8,128)S(1)} collective-permute-done((f32[3584,16]{0,1:T(8,128)S(1)}, f32[3584,16]{0,1:T(8,128)S(1)}, u32[]{:S(2)}, u32[]{:S(2)}) %collective-permute-start.1) | collective-permute-done | bytes 229408 | tf_op jit(solution)/shard_map/ppermute | solution.py:78
  199.9 0.7 add.47
  200.6 20.1 %reduce-scatter.2.cloned.1.call-done = f32[128,3584]{1,0:T(8,128)} async-done(((f32[512,3584]{1,0:T(8,128)}), f32[128,3584]{1,0:T(8,128)}) %reduce-scatter.2.cloned.1.call-update) | async-done | bytes 1835024 | tf_op jit(solution)/shard_map/reduce_scatter | solution.py:23
  220.7 2.5 convert_element_type.44
  223.3 71.7 %all-reduce.2.cloned.1.call-done = f32[16,2048]{1,0:T(8,128)} async-done(((f32[16,2048]{1,0:T(8,128)}), f32[16,2048]{1,0:T(8,128)}) %all-reduce.2.cloned.1.call-update) | async-done | bytes 131088 | tf_op jit(solution)/shard_map/psum | solution.py:75
  295.0 1.6 copy.11
  (21 shorter events, 0.2 us)
Async XLA Ops:
  7.2 118.2 %copy-start = (bf16[3584,16]{0,1:T(8,128)(2,1)S(1)}, bf16[3584,16]{0,1:T(8,128)(2,1)}, u32[]{:S(2)}) copy-start(bf16[3584,16]{0,1:T(8,128)(2,1)} %param.10) | copy-start | bytes 344068
  7.2 102.0 %all-gather.5.cloned.1.call-start = ((), (), s32[]{:S(2)}) async-start(), calls=%async_computation.2 | async-start | bytes 2359296 | tf_op jit(solution)/shard_map/all_gather | solution.py:57
  7.9 101.3 %all-gather.3.cloned.1.call-start = ((), (), s32[]{:S(2)}) async-start(), calls=%async_computation.1 | async-start | bytes 4587520 | tf_op jit(solution)/shard_map/all_gather | solution.py:35
  8.7 212.1 %reduce-scatter.2.cloned.1.call-start = ((), (), s32[]{:S(2)}) async-start(), calls=%async_computation.3 | async-start | bytes 9175040 | tf_op jit(solution)/shard_map/reduce_scatter | solution.py:23
  8.7 14.3 %slice-start = ((s8[7340032]{0:T(1024)(128)(4,1)}), s8[4194304]{0:T(1024)(128)(4,1)S(1)}, s32[]{:S(2)}) async-start(s8[7340032]{0:T(1024)(128)(4,1)} %bitcast.19), calls=%async_computation.5 | async-start | bytes 8388608
  16.5 6.5 %slice-start.1 = ((s8[7340032]{0:T(1024)(128)(4,1)}), s8[3145728]{0:T(1024)(128)(4,1)S(1)}, s32[]{:S(2)}) async-start(s8[7340032]{0:T(1024)(128)(4,1)} %bitcast.19), calls=%async_computation.6 | async-start | bytes 6291456
  109.2 16.2 %copy-start.2 = (bf16[16,2048]{1,0:T(8,128)(2,1)S(1)}, bf16[16,2048]{1,0:T(8,128)(2,1)}, u32[]{:S(2)}) copy-start(bf16[16,2048]{1,0:T(8,128)(2,1)} %param.11) | copy-start | bytes 196612
  109.2 16.2 %copy-start.3 = (bf16[512,2048]{1,0:T(8,128)(2,1)S(1)}, bf16[512,2048]{1,0:T(8,128)(2,1)}, u32[]{:S(2)}) copy-start(bf16[512,2048]{1,0:T(8,128)(2,1)} %all-gather.5.cloned.1.call-done) | copy-start | bytes 6291460
  147.0 148.0 %all-reduce.2.cloned.1.call-start = ((), (), s32[]{:S(2)}) async-start(), calls=%async_computation.4 | async-start | bytes 262144 | tf_op jit(solution)/shard_map/psum | solution.py:75
  174.4 14.3 %copy-start.1 = (bf16[3584,2048]{1,0:T(8,128)(2,1)S(1)}, bf16[3584,2048]{1,0:T(8,128)(2,1)}, u32[]{:S(2)}) copy-start(bf16[3584,2048]{1,0:T(8,128)(2,1)} %multiply_convert_fusion) | copy-start | bytes 44040196
  183.6 1.5 collective-permute-start
  185.1 14.8 %collective-permute-start.1 = (f32[3584,16]{0,1:T(8,128)S(1)}, f32[3584,16]{0,1:T(8,128)S(1)}, u32[]{:S(2)}, u32[]{:S(2)}) collective-permute-start(f32[3584,16]{0,1:T(8,128)S(1)} %add.46), channel_id=1, source_target_pairs={{0,2},{1,3},{2,0},{3,1},{4,6},{5,7},{6,4},{7,5},{8,10},{9,11},{10,... | collective-permute-start | bytes 688136 | tf_op jit(solution)/shard_map/ppermute | solution.py:78
Sparse Core Ops, SparseCore 0:
  10.1 51.7 all-gather.4
  63.5 29.9 all-gather.2
  147.1 73.5 reduce-scatter.1
  224.5 70.3 all-reduce.1
